TPU v7x, 256 devices: a whole 4x4x8 slice. The times are simulated.
256 devices in a mesh: site: 2 (over core), wide: 32 (over x, z), narrow: 4 (over y).
Axes of the slice: x: 4, y: 4, z: 8, core: 2. Of those that a mesh axis runs over, the one named last changes fastest.
Arguments:
- initial_rows: float32 [64, 4, 2048], P('site', 'narrow'), may hold values from -6 to 6
- outcomes: int32 [64, 4], replicated, may hold values 0 or 1
- tensors: float32 [4, 2, 4, 2048, 8192], P('site', None, 'narrow', None, 'wide'), may hold values from -0.25 to 0.25
Outputs:
- final_rows: float32 [64, 4, 2048], P('site', 'narrow')
- log_weight: float32 [64], P('site')
All inputs are finite; a program needn't handle non-finite values.
Results may differ from a plain program's by a relative error of at most 0.0003.
Values sent between devices are 32-bit elements; how exact they have to be, the bound alone decides.
A program may use at most 64 MiB of HBM per device.

v0:
```python
import jax
import jax.numpy as jnp
from jax import lax
from jax.sharding import PartitionSpec as P

BOND = 8192


epsilon = 1e-06
highest = lax.Precision.HIGHEST


def from_partner(value, axis, distance):
    mask = 2**distance
    pairs = [(source, source ^ mask) for source in range(lax.axis_size(axis))]
    return lax.ppermute(value, axis, pairs)


def advance(held, log_sum, site_tensor, chosen):
    front = held.shape[0]
    groups = lax.axis_size("narrow")
    share = front // groups
    summed = lax.psum_scatter(
        jnp.einsum(
            "bar,oard->bod",
            held,
            site_tensor,
            precision=highest,
            preferred_element_type=jnp.float32,
        ),
        "narrow",
        scatter_dimension=0,
        tiled=True,
    )
    local_choice = lax.dynamic_slice_in_dim(chosen, lax.axis_index("narrow") * share, share, 0)
    squares = jnp.sum(summed * summed, axis=2)
    raw_kept = jnp.where(local_choice[:, None] == 0, summed[:, 0, :], summed[:, 1, :])
    totals = lax.psum(squares, "wide")
    both_mean = (totals[:, 0] + totals[:, 1]) / (2.0 * BOND)
    scale = lax.rsqrt(both_mean + epsilon)
    full_rows = lax.all_gather(raw_kept * scale[:, None], "wide", axis=1, tiled=True)
    kept_square = jnp.where(local_choice == 0, totals[:, 0], totals[:, 1])
    local_ratio = jnp.log(kept_square / BOND + epsilon) - jnp.log(both_mean + epsilon)
    ratio_table = jnp.broadcast_to(local_ratio[:, None], (share, groups))
    split_rows = full_rows.reshape(share, groups, -1)
    moved, moved_ratio = (
        lax.all_to_all(split_rows, "narrow", split_axis=1, concat_axis=0, tiled=True),
        lax.all_to_all(ratio_table, "narrow", split_axis=1, concat_axis=0, tiled=True),
    )
    return (moved, log_sum + moved_ratio[:, 0])


def run_section(held, log_sum, tensors, chosen_block):
    for local_site in range(tensors.shape[0]):
        held, log_sum = advance(held, log_sum, tensors[local_site], chosen_block[:, local_site])
    return (held, log_sum)


def hand_over(held, log_sum):
    moved_rows, moved_sum = from_partner((held, log_sum), "site", 0)
    return (moved_rows, moved_sum)


def shards(initial_rows, outcomes, tensors):
    section = lax.axis_index("site")
    front = initial_rows.shape[0]
    local_count = tensors.shape[0]
    section_columns = lax.dynamic_slice_in_dim(outcomes, section * local_count, local_count, 1)
    held = initial_rows
    log_sum = jnp.zeros((front,), jnp.float32)
    front_order = (section, 1 - section, section)
    for turn_index in range(3):
        new_rows, new_sum = run_section(
            held,
            log_sum,
            tensors,
            lax.dynamic_slice_in_dim(section_columns, front_order[turn_index] * front, front, 0),
        )
        if turn_index == 1:
            held, log_sum = (new_rows, new_sum)
        else:
            active = section == 0 if turn_index == 0 else section == 1
            held = jnp.where(active, new_rows, held)
            log_sum = jnp.where(active, new_sum, log_sum)
        if turn_index < 2:
            held, log_sum = hand_over(held, log_sum)
    return (held, log_sum)


def solution(mesh):
    placed = (P("site", "narrow", None), P(), P("site", None, "narrow", None, "wide"))
    return jax.shard_map(
        shards,
        mesh=mesh,
        in_specs=placed,
        out_specs=(P("site", "narrow", None), P("site")),
        check_vma=False,
    )
```

profile of v0, /device:TPU:8, one launch (start us, length us, event | category | flops | bytes accessed | tf_op | source)
XLA Modules:
  0.0 992.5 jit_solution(1777501969221541964)
XLA Ops:
  7.2 5.4 fusion.2
  12.7 0.8 fusion.33
  13.6 23.4 %reduce-scatter.7.cloned.1.call-done = f32[8,2,256]{2,0,1:T(8,128)} async-done(((f32[32,2,256]{2,0,1:T(8,128)}), f32[8,2,256]{2,0,1:T(8,128)}) %reduce-scatter.7.cloned.1.call-update) | async-done | bytes 16400 | tf_op jit(solution)/shard_map/reduce_scatter | solution.py:23
  37.0 0.8 multiply_reduce_fusion.5
  37.9 75.1 %psum.42 = f32[8,2]{0,1:T(2,128)S(1)} all-reduce(f32[8,2]{0,1:T(2,128)S(1)} %multiply_reduce_fusion.5), channel_id=1, replica_groups=mesh['site'=2,'wide'=32,'narrow'=4] {'wide'}, use_global_device_ids=true, to_apply=%region_2.3 | all-reduce | flops 16 | bytes 128 | tf_op jit(solution)/shard_map/psum | solution.py:38
  113.8 46.0 %all_gather.18 = f32[8,8192]{1,0:T(8,128)S(1)} all-gather(f32[8,256]{1,0:T(8,128)S(1)} %fusion.24), channel_id=1, replica_groups=mesh['site'=2,'wide'=32,'narrow'=4] {'wide'}, dimensions={1}, use_global_device_ids=true | all-gather | bytes 270336 | tf_op jit(solution)/shard_map/all_gather | solution.py:41
  159.9 10.1 %all_to_all.171 = f32[8,4,2048]{2,0,1:T(8,128)S(1)} all-to-all(f32[8,4,2048]{2,0,1:T(8,128)S(1)} %bitcast.183), channel_id=1, replica_groups=mesh['site'=2,'wide'=32,'narrow'=4] {'narrow'}, dimensions={1} | all-to-all | bytes 524288 | tf_op jit(solution)/shard_map/all_to_all | solution.py:47
  170.0 5.3 fusion.5
  175.3 17.7 %reduce-scatter.9.cloned.1.call-done = f32[8,2,256]{2,0,1:T(8,128)} async-done(((f32[32,2,256]{2,0,1:T(8,128)}), f32[8,2,256]{2,0,1:T(8,128)}) %reduce-scatter.9.cloned.1.call-update) | async-done | bytes 16400 | tf_op jit(solution)/shard_map/reduce_scatter | solution.py:23
  193.1 0.8 multiply_reduce_fusion.4
  194.0 75.1 %psum.43 = f32[8,2]{0,1:T(2,128)S(1)} all-reduce(f32[8,2]{0,1:T(2,128)S(1)} %multiply_reduce_fusion.4), channel_id=1, replica_groups=mesh['site'=2,'wide'=32,'narrow'=4] {'wide'}, use_global_device_ids=true, to_apply=%region_5.6 | all-reduce | flops 16 | bytes 128 | tf_op jit(solution)/shard_map/psum | solution.py:38
  269.9 50.6 %all_gather.19 = f32[8,8192]{1,0:T(8,128)} all-gather(f32[8,256]{1,0:T(8,128)S(1)} %fusion.22), channel_id=1, replica_groups=mesh['site'=2,'wide'=32,'narrow'=4] {'wide'}, dimensions={1}, use_global_device_ids=true | all-gather | bytes 270336 | tf_op jit(solution)/shard_map/all_gather | solution.py:41
  320.5 5.8 all-to-all-start.1
  326.3 5.2 all-to-all-done.1
  331.7 1.5 collective-permute-done
  333.2 5.3 fusion.1
  338.6 17.2 %reduce-scatter.11.cloned.1.call-done = f32[8,2,256]{2,0,1:T(8,128)} async-done(((f32[32,2,256]{2,0,1:T(8,128)}), f32[8,2,256]{2,0,1:T(8,128)}) %reduce-scatter.11.cloned.1.call-update) | async-done | bytes 16400 | tf_op jit(solution)/shard_map/reduce_scatter | solution.py:23
  355.8 0.8 multiply_reduce_fusion.3
  356.7 75.0 %psum.44 = f32[8,2]{0,1:T(2,128)S(1)} all-reduce(f32[8,2]{0,1:T(2,128)S(1)} %multiply_reduce_fusion.3), channel_id=1, replica_groups=mesh['site'=2,'wide'=32,'narrow'=4] {'wide'}, use_global_device_ids=true, to_apply=%region_8.9 | all-reduce | flops 16 | bytes 128 | tf_op jit(solution)/shard_map/psum | solution.py:38
  432.6 46.0 %all_gather.20 = f32[8,8192]{1,0:T(8,128)S(1)} all-gather(f32[8,256]{1,0:T(8,128)S(1)} %fusion.20), channel_id=1, replica_groups=mesh['site'=2,'wide'=32,'narrow'=4] {'wide'}, dimensions={1}, use_global_device_ids=true | all-gather | bytes 270336 | tf_op jit(solution)/shard_map/all_gather | solution.py:41
  478.7 10.1 %all_to_all.172 = f32[8,4,2048]{2,0,1:T(8,128)S(1)} all-to-all(f32[8,4,2048]{2,0,1:T(8,128)S(1)} %bitcast.184), channel_id=1, replica_groups=mesh['site'=2,'wide'=32,'narrow'=4] {'narrow'}, dimensions={1} | all-to-all | bytes 524288 | tf_op jit(solution)/shard_map/all_to_all | solution.py:47
  488.8 5.3 fusion.4
  494.2 17.7 %reduce-scatter.13.cloned.1.call-done = f32[8,2,256]{2,0,1:T(8,128)} async-done(((f32[32,2,256]{2,0,1:T(8,128)}), f32[8,2,256]{2,0,1:T(8,128)}) %reduce-scatter.13.cloned.1.call-update) | async-done | bytes 16400 | tf_op jit(solution)/shard_map/reduce_scatter | solution.py:23
  512.8 75.0 %psum.45 = f32[8,2]{0,1:T(2,128)S(1)} all-reduce(f32[8,2]{0,1:T(2,128)S(1)} %multiply_reduce_fusion.2), channel_id=1, replica_groups=mesh['site'=2,'wide'=32,'narrow'=4] {'wide'}, use_global_device_ids=true, to_apply=%region_11.12 | all-reduce | flops 16 | bytes 128 | tf_op jit(solution)/shard_map/psum | solution.py:38
  588.7 46.0 %all_gather.21 = f32[8,8192]{1,0:T(8,128)S(1)} all-gather(f32[8,256]{1,0:T(8,128)S(1)} %fusion.18), channel_id=1, replica_groups=mesh['site'=2,'wide'=32,'narrow'=4] {'wide'}, dimensions={1}, use_global_device_ids=true | all-gather | bytes 270336 | tf_op jit(solution)/shard_map/all_gather | solution.py:41
  634.7 10.1 %all_to_all.173 = f32[8,4,2048]{2,0,1:T(8,128)S(1)} all-to-all(f32[8,4,2048]{2,0,1:T(8,128)S(1)} %bitcast.185), channel_id=1, replica_groups=mesh['site'=2,'wide'=32,'narrow'=4] {'narrow'}, dimensions={1} | all-to-all | bytes 524288 | tf_op jit(solution)/shard_map/all_to_all | solution.py:47
  644.9 1.5 collective-permute-done.1
  646.4 5.3 fusion
  651.7 7.6 all_to_all.174
  659.9 4.6 all-to-all-start.7
  664.5 3.7 all-to-all-done.7
  668.3 1.1 reduce-scatter.15.cloned.1.call-done
  670.9 5.6 all-to-all-start.8
  676.5 75.0 %psum.46 = f32[8,2]{0,1:T(2,128)S(1)} all-reduce(f32[8,2]{0,1:T(2,128)S(1)} %multiply_reduce_fusion.1), channel_id=1, replica_groups=mesh['site'=2,'wide'=32,'narrow'=4] {'wide'}, use_global_device_ids=true, to_apply=%region_14.15 | all-reduce | flops 16 | bytes 128 | tf_op jit(solution)/shard_map/psum | solution.py:38
  753.0 4.8 all-to-all-start.9
  757.8 50.6 %all_gather.22 = f32[8,8192]{1,0:T(8,128)} all-gather(f32[8,256]{1,0:T(8,128)S(1)} %fusion.16), channel_id=1, replica_groups=mesh['site'=2,'wide'=32,'narrow'=4] {'wide'}, dimensions={1}, use_global_device_ids=true | all-gather | bytes 270336 | tf_op jit(solution)/shard_map/all_gather | solution.py:41
  808.4 4.8 all-to-all-start.4
  813.4 5.0 all-to-all-done.4
  818.4 5.3 fusion.3
  824.3 4.6 all-to-all-start.10
  828.9 3.7 all-to-all-done.10
  832.6 8.4 reduce-scatter.17.cloned.1.call-done
  841.9 75.0 %psum.47 = f32[8,2]{0,1:T(2,128)S(1)} all-reduce(f32[8,2]{0,1:T(2,128)S(1)} %multiply_reduce_fusion), channel_id=1, replica_groups=mesh['site'=2,'wide'=32,'narrow'=4] {'wide'}, use_global_device_ids=true, to_apply=%region_17.18 | all-reduce | flops 16 | bytes 128 | tf_op jit(solution)/shard_map/psum | solution.py:38
  917.6 5.6 all-to-all-start.11
  924.0 50.6 %all_gather.23 = f32[8,8192]{1,0:T(8,128)} all-gather(f32[8,256]{1,0:T(8,128)S(1)} %fusion.14), channel_id=1, replica_groups=mesh['site'=2,'wide'=32,'narrow'=4] {'wide'}, dimensions={1}, use_global_device_ids=true | all-gather | bytes 270336 | tf_op jit(solution)/shard_map/all_gather | solution.py:41
  974.6 4.8 all-to-all-start.5
  980.0 4.6 all-to-all-done.5
  984.7 1.0 copy.12
  (64 shorter events, 12.5 us)
Async XLA Ops:
  7.2 324.4 %copy-start = (f32[32,1,2048]{2,1,0:T(1,128)S(1)}, f32[32,1,2048]{2,1,0:T(1,128)}, u32[]{:S(2)}) copy-start(f32[32,1,2048]{2,1,0:T(1,128)} %param.3) | copy-start | bytes 786436
  7.2 29.9 %reduce-scatter.7.cloned.1.call-start = ((), (), s32[]{:S(2)}) async-start(), calls=%async_computation.18 | async-start | bytes 81920 | tf_op jit(solution)/shard_map/reduce_scatter | solution.py:23
  12.7 180.4 %reduce-scatter.9.cloned.1.call-start = ((), (), s32[]{:S(2)}) async-start(), calls=%async_computation.19 | async-start | bytes 81920 | tf_op jit(solution)/shard_map/reduce_scatter | solution.py:23
  320.5 11.0 %all-to-all-start.1 = ((f32[8,4,2048]{2,0,1:T(8,128)}), f32[8,4,2048]{2,0,1:T(8,128)S(1)}, u32[]{:S(2)}, u32[]{:S(2)}) async-start(f32[8,4,2048]{2,0,1:T(8,128)} %bitcast.19), calls=%async_computation.3 | async-start | bytes 524288 | tf_op jit(solution)/shard_map/all_to_all | solution.py:47
  326.3 29.5 %reduce-scatter.11.cloned.1.call-start = ((), (), s32[]{:S(2)}) async-start(), calls=%async_computation.20 | async-start | bytes 81920 | tf_op jit(solution)/shard_map/reduce_scatter | solution.py:23
  331.6 1.6 collective-permute-start
  338.6 173.3 %reduce-scatter.13.cloned.1.call-start = ((), (), s32[]{:S(2)}) async-start(), calls=%async_computation.21 | async-start | bytes 81920 | tf_op jit(solution)/shard_map/reduce_scatter | solution.py:23
  494.1 175.3 %reduce-scatter.15.cloned.1.call-start = ((), (), s32[]{:S(2)}) async-start(), calls=%async_computation.22 | async-start | bytes 81920 | tf_op jit(solution)/shard_map/reduce_scatter | solution.py:23
  644.9 1.5 collective-permute-start.1
  659.9 8.3 all-to-all-start.7
  668.3 155.4 %collective-permute-start.2 = (f32[32]{0:T(128)S(1)}, f32[32]{0:T(128)S(1)}, u32[]{:S(2)}, u32[]{:S(2)}) collective-permute-start(f32[32]{0:T(128)S(1)} %select_n.125), channel_id=1, source_target_pairs={{0,128},{128,0},{1,129},{129,1},{2,130},{130,2},{3,131},{131,3},{4... | collective-permute-start | bytes 392 | tf_op jit(solution)/shard_map/ppermute | solution.py:16
  670.9 81.5 %all-to-all-start.8 = ((f32[8,4,1]{0,2,1:T(1,128)}), f32[8,4,1]{0,2,1:T(1,128)S(1)}, u32[]{:S(2)}, u32[]{:S(2)}) async-start(f32[8,4,1]{0,2,1:T(1,128)} %broadcast_in_dim.99), calls=%async_computation.14 | async-start | bytes 4096 | tf_op jit(solution)/shard_map/all_to_all | solution.py:48
  753.0 55.4 %all-to-all-start.9 = ((f32[8,4,1]{0,2,1:T(1,128)}), f32[8,4,1]{0,2,1:T(1,128)S(1)}, u32[]{:S(2)}, u32[]{:S(2)}) async-start(f32[8,4,1]{0,2,1:T(1,128)} %broadcast_in_dim.100), calls=%async_computation.15 | async-start | bytes 4096 | tf_op jit(solution)/shard_map/all_to_all | solution.py:48
  808.4 10.0 %all-to-all-start.4 = ((f32[8,4,2048]{2,0,1:T(8,128)}), f32[8,4,2048]{2,0,1:T(8,128)S(1)}, u32[]{:S(2)}, u32[]{:S(2)}) async-start(f32[8,4,2048]{2,0,1:T(8,128)} %bitcast.45), calls=%async_computation.9 | async-start | bytes 524288 | tf_op jit(solution)/shard_map/all_to_all | solution.py:47
  813.2 27.8 %reduce-scatter.17.cloned.1.call-start = ((), (), s32[]{:S(2)}) async-start(), calls=%async_computation.23 | async-start | bytes 81920 | tf_op jit(solution)/shard_map/reduce_scatter | solution.py:23
  824.3 8.3 all-to-all-start.10
  828.9 150.6 %collective-permute-start.3 = (f32[32]{0:T(128)S(1)}, f32[32]{0:T(128)S(1)}, u32[]{:S(2)}, u32[]{:S(2)}) collective-permute-start(f32[32]{0:T(128)S(1)} %add_add_fusion), channel_id=1, source_target_pairs={{0,128},{128,0},{1,129},{129,1},{2,130},{130,2},{3,131},{131,3},{4... | collective-permute-start | bytes 392 | tf_op jit(solution)/shard_map/ppermute | solution.py:16
  917.6 57.0 %all-to-all-start.11 = ((f32[8,4,1]{0,2,1:T(1,128)}), f32[8,4,1]{0,2,1:T(1,128)S(1)}, u32[]{:S(2)}, u32[]{:S(2)}) async-start(f32[8,4,1]{0,2,1:T(1,128)} %broadcast_in_dim.102), calls=%async_computation.17 | async-start | bytes 4096 | tf_op jit(solution)/shard_map/all_to_all | solution.py:48
  974.6 10.0 %all-to-all-start.5 = ((f32[8,4,2048]{2,0,1:T(8,128)}), f32[8,4,2048]{2,0,1:T(8,128)S(1)}, u32[]{:S(2)}, u32[]{:S(2)}) async-start(f32[8,4,2048]{2,0,1:T(8,128)} %bitcast.53), calls=%async_computation.11 | async-start | bytes 524288 | tf_op jit(solution)/shard_map/all_to_all | solution.py:47
Sparse Core Ops, SparseCore 0:
  12.8 24.1 reduce-scatter.6
  175.5 17.5 reduce-scatter.8
  338.7 17.1 reduce-scatter.10
  494.3 17.5 reduce-scatter.12
  651.8 17.5 reduce-scatter.14
  823.9 17.1 reduce-scatter.16
where the time goes:
time: 995 us; the launch traced here: 992 us
  blocking collectives  778 us (78%)
  waiting for transfers between devices  111 us (11%)
  starting transfers between devices  40.8 us (4%)
  matrix products  31.9 us (3%)
  between operations  14.2 us (1%)
  other arithmetic  11 us (1%)
    psum x6, blocking collectives, advance(): totals = lax.psum(squares, 'wide')  450 us
    all_gather x6, blocking collectives, advance(): lax.all_gather(raw_kept * scale[:, None], 'wide', axis=1, tiled=True)  290 us
    reduce_scatter x6, waiting for transfers between devices, advance(): lax.psum_scatter(jnp.einsum('bar,oard->bod', held, site_tensor, precision...  85.6 us
    dot_general x6, matrix products, advance(): jnp.einsum('bar,oard->bod', held, site_tensor, precision=highest, preferr...  31.9 us
    all_to_all x3, blocking collectives, advance(): lax.all_to_all(split_rows, 'narrow', split_axis=1, concat_axis=0, tiled=T...  30.4 us
    all_to_all x5, starting transfers between devices, advance(): lax.all_to_all(ratio_table, 'narrow', split_axis=1, concat_axis=0, tiled=...  25.2 us
  transfers between devices with their start and end apart: 18, of which 13 were waited for; matrix products, arithmetic and copies ran while one was open for 1% of the time, Pallas kernels for 0%

commit v1 on v0

v1 whole, which is shorter than its diff:
```python
import functools

import jax
import jax.numpy as jnp
from jax import lax
from jax.experimental import pallas as pl
from jax.experimental.pallas import tpu as pltpu
from jax.sharding import PartitionSpec as P

MESH = pl.DeviceIdType.MESH
EPSILON = 1e-06
STEPS = 4
BLOCK = 256
GROUP = 16
HALF = 8
LANES = 128


def split_value(value):
    high = value.astype(jnp.bfloat16)
    low = (value - high.astype(jnp.float32)).astype(jnp.bfloat16)
    return high, low


def near_first(extent):
    return sorted(range(1, extent), key=lambda d: min(d, extent - d))


def kernel(
    xn,
    zn,
    bond,
    x_hbm,
    oc_ref,
    t_hbm,
    raw_ref,
    aux_ref,
    t32,
    thi,
    tlo,
    xin,
    psend,
    rsb,
    st,
    stf,
    yex,
    yexf,
    ysend,
    t_sem,
    x_sem,
    f_sem,
    rs_send,
    rs_recv,
    z_send,
    z_recv,
    x_send,
    x_recv,
    y_send,
    y_recv,
):
    s = lax.axis_index("site")
    w = lax.axis_index("wide")
    y = lax.axis_index("narrow")
    x = lax.div(w, zn)
    z = lax.rem(w, zn)
    fronts = xn * HALF
    z_order = near_first(zn)

    def dev(site, xx, yy, zz):
        return (site, xx * zn + zz, yy)

    def around(value, offset, extent):
        return lax.rem(value + offset, extent)

    def remote(src, dst, send, recv, where):
        return pltpu.make_async_remote_copy(
            src_ref=src, dst_ref=dst, send_sem=send, recv_sem=recv, device_id=where, device_id_type=MESH
        )

    rows_k = zn * BLOCK
    t_chunk = min(rows_k, 512)
    chunks = rows_k // t_chunk

    def t_copy(site, c):
        rows = pl.ds(c * t_chunk, t_chunk)
        return pltpu.make_async_copy(t_hbm.at[site, :, 0, rows, :], t32.at[site, :, rows, :], t_sem.at[site, c])

    for c in range(chunks):
        t_copy(0, c).start()
    own_rows = pltpu.make_async_copy(x_hbm, xin.at[0], x_sem)

    @pl.when(s == 0)
    def _():
        own_rows.start()

    for c in range(chunks):
        t_copy(1, c).start()

    barrier = pltpu.get_barrier_semaphore()
    peers = 0
    for ds in range(2):
        for dx in range(xn):
            for dy in range(xn):
                if ds or dx or dy:
                    pl.semaphore_signal(
                        barrier,
                        inc=1,
                        device_id=dev(around(s, ds, 2), around(x, dx, xn), around(y, dy, xn), z),
                        device_id_type=MESH,
                    )
                    peers += 1
    for d in range(1, zn):
        pl.semaphore_signal(barrier, inc=1, device_id=dev(s, x, y, around(z, d, zn)), device_id_type=MESH)
        peers += 1
    pl.semaphore_wait(barrier, peers)

    def split_rows(site, start):
        for o in range(2):
            rows = pl.ds(start, BLOCK)
            high, low = split_value(t32[site, o, rows, :])
            thi[site, o, rows, :] = high
            tlo[site, o, rows, :] = low

    def block_product(lhs, site, start):
        high, low = split_value(lhs)
        both = jnp.concatenate([high, low], axis=0)
        n = lhs.shape[0]
        rows = pl.ds(start, BLOCK)
        out = []
        for o in range(2):
            t_high, t_low = thi[site, o, rows, :], tlo[site, o, rows, :]
            main = jnp.dot(both, t_high, preferred_element_type=jnp.float32)
            rest = jnp.dot(high, t_low, preferred_element_type=jnp.float32)
            out.append(main[:n] + (main[n:] + rest))
        return out

    def put_product(k, total):
        for g in range(xn):
            for o in range(2):
                psend[k, g, :, o * BLOCK : (o + 1) * BLOCK] = total[o][g * GROUP : (g + 1) * GROUP]

    def reduce_sends(k, same_core, target):
        waits = []
        for dg in range(xn):
            g = around(x, dg, xn)
            if k < 3:
                copy = remote(
                    psend.at[k, g], rsb.at[k, y], rs_send.at[k, dg, 0], rs_recv.at[k, y], dev(target, g, x, z)
                )
                if dg == 0 and same_core:
                    here = pltpu.make_async_copy(psend.at[k, g], rsb.at[k, y], rs_recv.at[k, y])
                    pl.when(x == y)(here.start)
                    pl.when(x != y)(copy.start)
                    waits.append(functools.partial(pl.when(x != y), copy.wait_send))
                else:
                    copy.start()
                    waits.append(copy.wait_send)
            else:
                for f in range(2):
                    part = pl.ds(f * HALF, HALF)
                    src, dst = psend.at[k, g, part, :], rsb.at[k, y, pl.ds(0, HALF), :]
                    copy = remote(src, dst, rs_send.at[k, dg, f], rs_recv.at[k, y], dev(f, g, x, z))
                    if dg == 0 and f == 1:
                        here = pltpu.make_async_copy(src, dst, rs_recv.at[k, y])
                        pl.when(x == y)(here.start)
                        pl.when(x != y)(copy.start)
                        waits.append(functools.partial(pl.when(x != y), copy.wait_send))
                    else:
                        copy.start()
                        waits.append(copy.wait_send)
        return waits

    def choices(k):
        own = oc_ref[pl.ds(pl.multiple_of(x * HALF, HALF), HALF), :]
        other = oc_ref[pl.ds(pl.multiple_of(fronts + x * HALF, HALF), HALF), :]
        return jnp.concatenate([own, other], axis=0)[:, k : k + 1]

    def weigh(total, chosen):
        first, second = total[:, 0:1], total[:, 32:33]
        both_mean = (first + second) / (2.0 * bond)
        kept_square = jnp.where(chosen == 0, first, second)
        scale = lax.rsqrt(both_mean + EPSILON)
        ratio = jnp.log(kept_square / bond + EPSILON) - jnp.log(both_mean + EPSILON)
        return scale, total[:, 64:65] + ratio

    def wait_tiles(k, same_core):
        for dy in range(xn):
            y2 = around(y, dy, xn)
            if dy == 0 and same_core:
                continue
            slot = yex.at[k, y2] if k < 3 else yexf.at[y2]
            remote(slot, slot, y_send.at[k, 0], y_recv.at[k, y2], dev(s, x, y, z)).wait_recv()

    def sum_slots(ref, rows):
        total = ref[0, rows, :]
        for j in range(1, xn):
            total = total + ref[j, rows, :]
        return total

    def reduce_group(k, rows, scale, chosen, log_sum):
        for dy in range(xn):
            j = around(y, dy, xn)
            slot = rsb.at[k, j] if k < 3 else rsb.at[k, j, pl.ds(0, HALF), :]
            remote(slot, slot, rs_send.at[k, 0, 0], rs_recv.at[k, j], dev(s, x, y, z)).wait_recv()
        total = sum_slots(rsb.at[k], pl.ds(0, rows))
        if scale is not None:
            total = total * scale
        first, second = total[:, :BLOCK], total[:, BLOCK:]
        square_first = jnp.sum(first * first, axis=1, keepdims=True)
        square_second = jnp.sum(second * second, axis=1, keepdims=True)
        kept = jnp.where(chosen == 0, first, second)
        lane = lax.broadcasted_iota(jnp.int32, (rows, LANES), 1)
        carried = jnp.where((lane >= 64) & (y == 0) & (z == 0), log_sum, 0.0)
        tile = jnp.where(lane < 32, square_first, jnp.where(lane < 64, square_second, carried))
        block = st.at[k, z, x] if k < 3 else stf.at[z, x]
        block[0] = kept[:, :LANES]
        block[1] = kept[:, LANES:]
        block[2] = tile

    def gather(k):
        waits = []
        blocks = st.at[k] if k < 3 else stf
        sub = 2 if k < 3 else 3

        def pass_on(d, z2):
            for dx in range(1, xn):
                part = blocks.at[z2, x, pl.ds(0, sub)]
                copy = remote(
                    part, part, x_send.at[k, d, dx], x_recv.at[k, z2, x], dev(s, around(x, dx, xn), y, z)
                )
                copy.start()
                waits.append(copy.wait_send)

        for d in z_order:
            copy = remote(
                blocks.at[z, x],
                blocks.at[z, x],
                z_send.at[k, d],
                z_recv.at[k, z],
                dev(s, x, y, around(z, d, zn)),
            )
            copy.start()
            waits.append(copy.wait_send)
        pass_on(0, z)
        for d in z_order:
            z2 = around(z, d, zn)
            block = blocks.at[z2, x]
            remote(block, block, z_send.at[k, d], z_recv.at[k, z2], dev(s, x, y, z)).wait_recv()
            pass_on(d, z2)
        return waits

    def wait_block(k, z2):
        blocks = st.at[k] if k < 3 else stf
        sub = 2 if k < 3 else 3
        for dx in range(1, xn):
            part = blocks.at[z2, around(x, dx, xn), pl.ds(0, sub)]
            remote(
                part, part, x_send.at[k, 0, dx], x_recv.at[k, z2, around(x, dx, xn)], dev(s, x, y, z)
            ).wait_recv()

    def tile_sends(k, same_core, targets):
        waits = []
        total = st[k, 0, x, 2]
        for j in range(1, zn):
            total = total + st[k, j, x, 2]
        ysend[k] = total
        if same_core:
            yex[k, y] = total
        for index, target in enumerate(targets):
            for dy in range(xn):
                if dy == 0 and same_core and target == 1:
                    continue
                copy = remote(
                    ysend.at[k],
                    yex.at[k, y],
                    y_send.at[k, index * xn + dy],
                    y_recv.at[k, y],
                    dev(target, x, around(y, dy, xn), z),
                )
                copy.start()
                waits.append(copy.wait_send)
        return waits

    def gathered_product(k, site):
        total = None
        for d in [0] + z_order:
            z2 = around(z, d, zn)
            wait_block(k, z2)
            lhs = jnp.concatenate(
                [jnp.concatenate([st[k, z2, g, 0], st[k, z2, g, 1]], axis=1) for g in range(xn)], axis=0
            )
            out = block_product(lhs, site, pl.multiple_of(z2 * BLOCK, BLOCK))
            total = out if total is None else [total[0] + out[0], total[1] + out[1]]
        return total

    def wait_all(waits):
        for wait in waits:
            wait()

    partner_rows = remote(x_hbm, xin.at[1], f_sem.at[0], f_sem.at[1], dev(around(s, 1, 2), x, y, z))

    @pl.when(s == 0)
    def _():
        waits = []
        own_rows.wait()
        for c in range(chunks):
            t_copy(0, c).wait()
            for b in range(t_chunk // BLOCK):
                split_rows(0, c * t_chunk + b * BLOCK)
        partner_rows.wait_recv()
        total = None
        width = BLOCK // LANES
        stride = zn * width
        for kb in range(zn):
            pieces = []
            for g in range(xn):
                for f in range(2):
                    pieces.append(
                        jnp.concatenate(
                            [
                                xin[f, pl.ds(g * HALF * stride + kb * width + c, HALF, stride=stride), :]
                                for c in range(width)
                            ],
                            axis=1,
                        )
                    )
            out = block_product(jnp.concatenate(pieces, axis=0), 0, kb * BLOCK)
            total = out if total is None else [total[0] + out[0], total[1] + out[1]]
        put_product(0, total)
        waits += reduce_sends(0, True, 0)
        for c in range(chunks):
            t_copy(1, c).wait()
            for b in range(t_chunk // BLOCK):
                split_rows(1, c * t_chunk + b * BLOCK)
        reduce_group(0, GROUP, None, choices(0), 0.0)
        waits += gather(0)
        waits += tile_sends(0, False, (1,))
        put_product(1, gathered_product(0, 1))
        waits += reduce_sends(1, False, 1)
        wait_all(waits)
        wait_tiles(2, False)

    @pl.when(s == 1)
    def _():
        waits = []
        partner_rows.start()
        waits.append(partner_rows.wait_send)
        for site in range(2):
            for c in range(chunks):
                t_copy(site, c).wait()
                for b in range(t_chunk // BLOCK):
                    split_rows(site, c * t_chunk + b * BLOCK)
        wait_tiles(0, False)
        scale, logs = weigh(sum_slots(yex.at[0], pl.ds(0, GROUP)), choices(0))
        reduce_group(1, GROUP, scale, choices(1), 0.0)
        waits += gather(1)
        waits += tile_sends(1, True, (1,))
        put_product(2, gathered_product(1, 0))
        waits += reduce_sends(2, True, 1)
        wait_tiles(1, True)
        scale, more = weigh(sum_slots(yex.at[1], pl.ds(0, GROUP)), choices(1))
        reduce_group(2, GROUP, scale, choices(2), logs + more)
        waits += gather(2)
        waits += tile_sends(2, True, (1, 0))
        put_product(3, gathered_product(2, 1))
        waits += reduce_sends(3, True, 1)
        wait_all(waits)
        wait_tiles(2, True)

    mine = oc_ref[pl.ds(pl.multiple_of(s * fronts, HALF), fronts), :]
    group_rows = pl.ds(pl.multiple_of(s * fronts + x * HALF, HALF), HALF)
    chosen = oc_ref[group_rows, :]
    scale, logs = weigh(sum_slots(yex.at[2], pl.ds(pl.multiple_of(s * HALF, HALF), HALF)), chosen[:, 2:3])
    reduce_group(3, HALF, scale, chosen[:, 3:4], logs)
    waits = gather(3)
    parts = []
    for d in [0] + z_order:
        z2 = around(z, d, zn)
        wait_block(3, z2)
        for g in range(xn):
            for c in range(2):
                column = pl.ds(pl.multiple_of(z2 * BLOCK + c * LANES, LANES), LANES)
                raw_ref[g * HALF : (g + 1) * HALF, column] = stf[z2, g, c]
    for g in range(xn):
        tile = stf[0, g, 2]
        for j in range(1, zn):
            tile = tile + stf[j, g, 2]
        parts.append(tile)
    total = jnp.concatenate(parts, axis=0)
    yexf[y] = total
    for dy in range(1, xn):
        copy = remote(
            yexf.at[y], yexf.at[y], y_send.at[3, dy], y_recv.at[3, y], dev(s, x, around(y, dy, xn), z)
        )
        copy.start()
        waits.append(copy.wait_send)
    wait_tiles(3, True)
    scale, logs = weigh(sum_slots(yexf, pl.ds(0, fronts)), mine[:, 3:4])
    lane = lax.broadcasted_iota(jnp.int32, (fronts, LANES), 1)
    aux_ref[...] = jnp.where(lane < 64, scale, logs)
    wait_all(waits)


def shards(xn, zn, initial_rows, outcomes, tensors):
    fronts, _, rows_k = initial_rows.shape
    bond = xn * rows_k
    dma = pltpu.SemaphoreType.DMA
    vmem = pl.BlockSpec(memory_space=pltpu.VMEM)
    anywhere = pl.BlockSpec(memory_space=pl.ANY)
    f32 = jnp.float32
    raw, aux = pl.pallas_call(
        functools.partial(kernel, xn, zn, float(bond)),
        out_shape=(
            jax.ShapeDtypeStruct((fronts, rows_k), f32),
            jax.ShapeDtypeStruct((fronts, LANES), f32),
        ),
        in_specs=[anywhere, vmem, anywhere],
        out_specs=(vmem, vmem),
        scratch_shapes=[
            pltpu.VMEM((2, 2, rows_k, BLOCK), f32),
            pltpu.VMEM((2, 2, rows_k, BLOCK), jnp.bfloat16),
            pltpu.VMEM((2, 2, rows_k, BLOCK), jnp.bfloat16),
            pltpu.VMEM((2, fronts * rows_k // LANES, LANES), f32),
            pltpu.VMEM((STEPS, xn, GROUP, 2 * BLOCK), f32),
            pltpu.VMEM((STEPS, xn, GROUP, 2 * BLOCK), f32),
            pltpu.VMEM((3, zn, xn, 3, GROUP, LANES), f32),
            pltpu.VMEM((zn, xn, 3, HALF, LANES), f32),
            pltpu.VMEM((3, xn, GROUP, LANES), f32),
            pltpu.VMEM((xn, fronts, LANES), f32),
            pltpu.VMEM((3, GROUP, LANES), f32),
            dma((2, max(1, rows_k // 512))),
            dma,
            dma((2,)),
            dma((STEPS, xn, 2)),
            dma((STEPS, xn)),
            dma((STEPS, zn)),
            dma((STEPS, zn)),
            dma((STEPS, zn, xn)),
            dma((STEPS, zn, xn)),
            dma((STEPS, 2 * xn)),
            dma((STEPS, xn)),
        ],
        compiler_params=pltpu.CompilerParams(
            collective_id=0, has_side_effects=True, vmem_limit_bytes=56 * 1024 * 1024
        ),
    )(initial_rows.reshape(fronts * rows_k // LANES, LANES), outcomes, tensors)
    rows = (raw * aux[:, :1])[:, None, :]
    return rows, aux[:, 64]


def solution(mesh):
    xn = mesh.shape["narrow"]
    zn = mesh.shape["wide"] // xn
    return jax.shard_map(
        functools.partial(shards, xn, zn),
        mesh=mesh,
        in_specs=(P("site", "narrow", None), P(), P("site", None, "narrow", None, "wide")),
        out_specs=(P("site", "narrow", None), P("site")),
        check_vma=False,
    )
```

time: 995 us -> 79.5 us (0.08)
  blocking collectives: 778 us -> 0 us
  waiting for transfers between devices: 111 us -> 0 us
  Pallas kernels: 0 us -> 73.1 us
  starting transfers between devices: 40.8 us -> 0 us
  matrix products: 31.9 us -> 0 us
  between operations: 14.2 us -> 0.64 us
  other arithmetic: 11 us -> 1.04 us
    psum x6 -> x0, blocking collectives: 450 us -> none  [advance(): totals = lax.psum(squares, 'wide')]
    all_gather x6 -> x0, blocking collectives: 290 us -> none  [advance(): lax.all_gather(raw_kept * scale[:, None], 'wide', axis=1, tiled=True)]
    reduce_scatter x6 -> x0, waiting for transfers between devices: 85.6 us -> none  [advance(): lax.psum_scatter(jnp.einsum('bar,oard->bod', held, site_tensor, precision...]
    pallas_call x0 -> x1, Pallas kernels: none -> 73.1 us  [shards(): pl.pallas_call(functools.partial(kernel, xn, zn, float(bond)), out_shape=...]
    all_to_all x8 -> x0, starting transfers between devices: 40.5 us -> none  [the longest x5 25.2 us: advance(): lax.all_to_all(ratio_table, 'narrow', split_axis=1, concat_axis=0, tiled=...]
    all_to_all x4 -> x0, blocking collectives: 38 us -> none  [the longest x3 30.4 us: advance(): lax.all_to_all(split_rows, 'narrow', split_axis=1, concat_axis=0, tiled=T...]
    dot_general x6 -> x0, matrix products: 31.9 us -> none  [advance(): jnp.einsum('bar,oard->bod', held, site_tensor, precision=highest, preferr...]
    all_to_all x8 -> x0, waiting for transfers between devices: 22.2 us -> none  [the longest x3 14.8 us: advance(): lax.all_to_all(split_rows, 'narrow', split_axis=1, concat_axis=0, tiled=T...]
  transfers between devices with their start and end apart: 18 -> 0, of which waited for: 13 -> 0; matrix products, arithmetic and copies ran while one was open for 1% -> 0% of each run, Pallas kernels for 0% -> 0%
where the time goes in v1:
time: 79.5 us; the launch traced here: 78.6 us
  Pallas kernels  73.1 us (92%)
  local copies, waits for them, and re-layouts  3.85 us (5%)
  other arithmetic  1.04 us (1%)
    pallas_call x1, Pallas kernels, shards(): pl.pallas_call(functools.partial(kernel, xn, zn, float(bond)), out_shape=...  73.1 us
    unnamed x2, local copies, waits for them, and re-layouts  2.36 us

profile of v1, /device:TPU:8, one launch (start us, length us, event | category | flops | bytes accessed | tf_op | source)
XLA Modules:
  0.0 78.6 jit_solution(3876469463703961901)
XLA Ops:
  0.6 1.4 %copy.7.oc_ref = s32[64,4]{1,0:T(8,128)} copy(s32[64,4]{0,1:T(4,128)} %param.4) | data formatting | bytes 2048 | tf_op args[1]
  2.0 73.1 %shard_map.50 = (f32[32,2048]{1,0:T(8,128)}, f32[32,128]{1,0:T(8,128)}) custom-call(f32[512,128]{1,0:T(8,128)} %bitcast.3, s32[64,4]{1,0:T(8,128)} %copy.7.oc_ref, f32[2,2,1,2048,256]{4,3,2,1,0:T(8,128)} %t_hbm.1), custom_call_target="tpu_custom_call" | custom-call | tf_op jit(solution)/shard_map/pallas_call | solution.py:411
  75.1 1.5 %slice_reduce_fusion = (f32[32]{0:T(128)}, f32[32]{0:T(128)S(1)}) fusion(f32[32,128]{1,0:T(8,128)} %get-tuple-element.5), kind=kLoop, calls=%fused_computation.1 | loop fusion | bytes 512 | tf_op jit(solution)/shard_map/slice | solution.py:448
  76.6 1.0 %multiply_bitcast_fusion = f32[32,1,2048]{2,0,1:T(8,128)S(1)} fusion(f32[32,2048]{1,0:T(8,128)} %get-tuple-element.4, f32[32]{0:T(128)S(1)} %get-tuple-element.11), kind=kLoop, calls=%fused_computation | loop fusion | flops 65536 | bytes 524416 | tf_op jit(solution)/shard_map/broadcast_in_dim | solution.py:447
  77.6 1.0 %copy.8 = f32[32,1,2048]{2,1,0:T(1,128)} copy(f32[32,1,2048]{2,0,1:T(8,128)S(1)} %multiply_bitcast_fusion) | data formatting | bytes 524288

commit v2 on v1

v2 whole, which is shorter than its diff:
```python
import functools

import jax
import jax.numpy as jnp
from jax import lax
from jax.experimental import pallas as pl
from jax.experimental.pallas import tpu as pltpu
from jax.sharding import PartitionSpec as P

MESH = pl.DeviceIdType.MESH
EPSILON = 1e-06
STEPS = 4
BLOCK = 256
GROUP = 16
HALF = 8
LANES = 128


def split_value(value):
    high = value.astype(jnp.bfloat16)
    low = (value - high.astype(jnp.float32)).astype(jnp.bfloat16)
    return high, low


def ring_distance(offset, extent):
    return min(offset, extent - offset)


def kernel(
    xn,
    zn,
    bond,
    x_hbm,
    oc_ref,
    t_hbm,
    rows_ref,
    log_ref,
    t32,
    thi,
    tlo,
    xin,
    psend,
    rsb,
    rsf,
    st,
    tl,
    stf,
    tlf,
    yex,
    yexf,
    ysend,
    tsend,
    t_sem,
    x_sem,
    rs_send,
    rs_recv,
    ag_send,
    ag_recv,
    y_send,
    y_recv,
    tl_recv,
):
    s = lax.axis_index("site")
    w = lax.axis_index("wide")
    y = lax.axis_index("narrow")
    x = lax.div(w, zn)
    z = lax.rem(w, zn)
    fronts = xn * HALF
    reach = zn // 2
    offsets = [(dz, dx) for dz in range(zn) for dx in range(xn) if dz or dx]
    offsets.sort(key=lambda o: -(ring_distance(o[0], zn) + ring_distance(o[1], xn)))

    def dev(site, xx, yy, zz):
        return (site, xx * zn + zz, yy)

    def around(value, offset, extent):
        return lax.rem(value + offset, extent)

    def remote(src, dst, send, recv, where):
        copy = pltpu.make_async_remote_copy(
            src_ref=src, dst_ref=dst, send_sem=send, recv_sem=recv, device_id=where, device_id_type=MESH
        )
        return copy

    def wait_kib(sem, kib):
        view = xin.at[0, pl.ds(0, 2 * kib), :] if kib % 8 else t32.at[0, 0, pl.ds(0, kib), :]
        pltpu.make_async_copy(view, view, sem).wait()

    rows_k = zn * BLOCK
    t_chunk = min(rows_k, 512)
    chunks = rows_k // t_chunk

    def t_copy(site, c):
        rows = pl.ds(c * t_chunk, t_chunk)
        return pltpu.make_async_copy(t_hbm.at[site, :, 0, rows, :], t32.at[site, :, rows, :], t_sem.at[site, c])

    own_rows = pltpu.make_async_copy(x_hbm, xin.at[0], x_sem.at[0])
    pl.when(s == 0)(own_rows.start)
    for site in range(2):
        for c in range(chunks):
            t_copy(site, c).start()

    barrier = pltpu.get_barrier_semaphore()
    peers = 0
    for ds in range(2):
        for dx in range(xn):
            for dy in range(xn):
                if ds or dx or dy:
                    where = dev(around(s, ds, 2), around(x, dx, xn), around(y, dy, xn), z)
                    pl.semaphore_signal(barrier, inc=1, device_id=where, device_id_type=MESH)
                    peers += 1
    for dz in range(1, zn):
        for dx in range(xn):
            where = dev(s, around(x, dx, xn), y, around(z, dz, zn))
            pl.semaphore_signal(barrier, inc=1, device_id=where, device_id_type=MESH)
            peers += 1
    pl.semaphore_wait(barrier, peers)

    def split_rows(site, start):
        for o in range(2):
            rows = pl.ds(start, BLOCK)
            high, low = split_value(t32[site, o, rows, :])
            thi[site, o, rows, :] = high
            tlo[site, o, rows, :] = low

    def split_chunk(site, c):
        t_copy(site, c).wait()
        for b in range(t_chunk // BLOCK):
            split_rows(site, c * t_chunk + b * BLOCK)

    def block_product(lhs, site, start):
        high, low = split_value(lhs)
        both = jnp.concatenate([high, low], axis=0)
        n = lhs.shape[0]
        rows = pl.ds(start, BLOCK)
        out = []
        for o in range(2):
            t_high, t_low = thi[site, o, rows, :], tlo[site, o, rows, :]
            main = jnp.dot(both, t_high, preferred_element_type=jnp.float32)
            rest = jnp.dot(high, t_low, preferred_element_type=jnp.float32)
            out.append(main[:n] + (main[n:] + rest))
        return out

    def put_product(k, total):
        for g in range(xn):
            for o in range(2):
                psend[k, g, :, o * BLOCK : (o + 1) * BLOCK] = total[o][g * GROUP : (g + 1) * GROUP]

    def reduce_sends(k, same_core, target):
        for dg in range(xn):
            g = around(x, dg, xn)
            for f in range(1 if k < 3 else 2):
                if k < 3:
                    src, dst, core = psend.at[k, g], rsb.at[k, y], target
                    here = dg == 0 and same_core
                else:
                    src, dst, core = psend.at[k, g, pl.ds(f * HALF, HALF), :], rsf.at[y], f
                    here = dg == 0 and f == 1
                copy = remote(src, dst, rs_send.at[k], rs_recv.at[k], dev(core, g, x, z))
                if here:
                    local = pltpu.make_async_copy(src, dst, rs_recv.at[k])
                    pl.when(x == y)(local.start)
                    pl.when(x != y)(copy.start)
                else:
                    copy.start()

    def end_reduce_sends(k, same_core):
        each = GROUP * 2 * BLOCK * 4 // 1024
        own = each if k < 3 else each // 2
        if same_core:
            pl.when(x == y)(lambda: wait_kib(rs_send.at[k], xn * each - own))
            pl.when(x != y)(lambda: wait_kib(rs_send.at[k], xn * each))
        else:
            wait_kib(rs_send.at[k], xn * each)

    def outcome_rows(k, rows, first_row):
        line = oc_ref[k : k + 1, :].astype(jnp.float32)
        shape = (rows, oc_ref.shape[1])
        lane = lax.broadcasted_iota(jnp.int32, shape, 1)
        row = lax.broadcasted_iota(jnp.int32, shape, 0)
        picked = jnp.where(lane == first_row(row), jnp.broadcast_to(line, shape), 0.0)
        return jnp.sum(picked, axis=1, keepdims=True) < 0.5

    def group_outcomes(k):
        return outcome_rows(
            k, GROUP, lambda row: x * HALF + jnp.where(row < HALF, row, row + (fronts - HALF))
        )

    def weigh(total, is_first):
        first, second = total[:, 0:1], total[:, 32:33]
        both_mean = (first + second) / (2.0 * bond)
        kept_square = jnp.where(is_first, first, second)
        scale = lax.rsqrt(both_mean + EPSILON)
        ratio = jnp.log(kept_square / bond + EPSILON) - jnp.log(both_mean + EPSILON)
        return scale, total[:, 64:65] + ratio

    def tree(items):
        items = list(items)
        while len(items) > 1:
            items = [sum(items[i : i + 2][1:], items[i]) for i in range(0, len(items), 2)]
        return items[0]

    def reduce_group(k, scale, is_first, log_sum):
        buffer = rsb.at[k] if k < 3 else rsf
        rows = GROUP if k < 3 else HALF
        wait_kib(rs_recv.at[k], xn * rows * 2 * BLOCK * 4 // 1024)
        total = tree(buffer[j] for j in range(xn))
        if scale is not None:
            total = total * scale
        first, second = total[:, :BLOCK], total[:, BLOCK:]
        kept = jnp.where(is_first, first, second)
        block = st.at[k, z, x] if k < 3 else stf.at[z, x]
        block[0] = kept[:, :LANES]
        block[1] = kept[:, LANES:]
        for dz, dx in offsets:
            copy = remote(
                block,
                block,
                ag_send.at[k],
                ag_recv.at[k, ring_distance(dz, zn)],
                dev(s, around(x, dx, xn), y, around(z, dz, zn)),
            )
            copy.start()
        square_first = jnp.sum(first * first, axis=1, keepdims=True)
        square_second = jnp.sum(second * second, axis=1, keepdims=True)
        lane = lax.broadcasted_iota(jnp.int32, (rows, LANES), 1)
        carried = jnp.where((lane >= 64) & (y == 0) & (z == 0), log_sum, 0.0)
        return jnp.where(lane < 32, square_first, jnp.where(lane < 64, square_second, carried))

    def end_gather_sends(k):
        each = (GROUP if k < 3 else HALF) * BLOCK * 4 // 1024
        wait_kib(ag_send.at[k], len(offsets) * each)

    def wait_blocks(k, distance):
        each = (GROUP if k < 3 else HALF) * BLOCK * 4 // 1024
        count = sum(1 for dz, dx in offsets if ring_distance(dz, zn) == distance)
        wait_kib(ag_recv.at[k, distance], count * each)

    tile_kib = GROUP * LANES * 4 // 1024

    def spread_tile(k, tile):
        tl[k, z] = tile
        for dz in range(1, zn):
            copy = remote(tl.at[k, z], tl.at[k, z], y_send.at[0], tl_recv.at[k], dev(s, x, y, around(z, dz, zn)))
            copy.start()

    def pass_tiles(k, same_core, targets):
        wait_kib(tl_recv.at[k], (zn - 1) * tile_kib)
        total = tree(tl[k, j] for j in range(zn))
        ysend[k] = total
        if same_core:
            yex[k, y] = total
        for target in targets:
            for dy in range(xn):
                if dy == 0 and same_core and target == 1:
                    continue
                where = dev(target, x, around(y, dy, xn), z)
                remote(ysend.at[k], yex.at[k, y], y_send.at[0], y_recv.at[k], where).start()

    def tile_total(k, same_core, rows):
        wait_kib(y_recv.at[k], (xn - 1 if same_core else xn) * tile_kib)
        return tree(yex[k, j, rows, :] for j in range(xn))

    def gathered_product(k, site):
        total = None
        for distance in range(reach + 1):
            wait_blocks(k, distance)
            for dz in sorted({distance, (zn - distance) % zn}):
                z2 = around(z, dz, zn)
                lhs = jnp.concatenate(
                    [jnp.concatenate([st[k, z2, g, 0], st[k, z2, g, 1]], axis=1) for g in range(xn)], axis=0
                )
                out = block_product(lhs, site, pl.multiple_of(z2 * BLOCK, BLOCK))
                total = out if total is None else [total[0] + out[0], total[1] + out[1]]
        return total

    partner_rows = remote(x_hbm, xin.at[1], x_sem.at[1], x_sem.at[2], dev(around(s, 1, 2), x, y, z))
    all_rows = pl.ds(0, GROUP)

    @pl.when(s == 0)
    def _():
        own_rows.wait()
        partner_rows.wait_recv()
        total = None
        width = BLOCK // LANES
        stride = zn * width
        for kb in range(zn):
            if kb % (t_chunk // BLOCK) == 0:
                split_chunk(0, kb * BLOCK // t_chunk)
            pieces = []
            for g in range(xn):
                for f in range(2):
                    pieces.append(
                        jnp.concatenate(
                            [
                                xin[f, pl.ds(g * HALF * stride + kb * width + c, HALF, stride=stride), :]
                                for c in range(width)
                            ],
                            axis=1,
                        )
                    )
            out = block_product(jnp.concatenate(pieces, axis=0), 0, kb * BLOCK)
            total = out if total is None else [total[0] + out[0], total[1] + out[1]]
        put_product(0, total)
        reduce_sends(0, True, 0)
        for c in range(chunks):
            split_chunk(1, c)
        spread_tile(0, reduce_group(0, None, group_outcomes(0), 0.0))
        put_product(1, gathered_product(0, 1))
        reduce_sends(1, False, 1)
        pass_tiles(0, False, (1,))
        end_reduce_sends(0, True)
        end_reduce_sends(1, False)
        end_gather_sends(0)
        wait_kib(y_send.at[0], (zn - 1 + xn) * tile_kib)
        yex[0, 0] = tile_total(2, False, all_rows)

    @pl.when(s == 1)
    def _():
        partner_rows.start()
        for site in range(2):
            for c in range(chunks):
                split_chunk(site, c)
        is_first = group_outcomes(0)
        scale, logs = weigh(tile_total(0, False, all_rows), is_first)
        is_first = group_outcomes(1)
        spread_tile(1, reduce_group(1, scale, is_first, 0.0))
        put_product(2, gathered_product(1, 0))
        reduce_sends(2, True, 1)
        pass_tiles(1, True, (1,))
        scale, more = weigh(tile_total(1, True, all_rows), is_first)
        logs = logs + more
        is_first = group_outcomes(2)
        spread_tile(2, reduce_group(2, scale, is_first, logs))
        put_product(3, gathered_product(2, 1))
        reduce_sends(3, True, 1)
        pass_tiles(2, True, (1, 0))
        partner_rows.wait_send()
        end_reduce_sends(2, True)
        end_reduce_sends(3, True)
        end_gather_sends(1)
        end_gather_sends(2)
        wait_kib(y_send.at[0], (2 * (zn - 1) + (xn - 1) + (2 * xn - 1)) * tile_kib)
        yex[0, 0] = tile_total(2, True, all_rows)

    before = yex[0, 0, pl.ds(pl.multiple_of(s * HALF, HALF), HALF), :]
    was_first = outcome_rows(2, HALF, lambda row: s * fronts + x * HALF + row)
    is_first = outcome_rows(3, HALF, lambda row: s * fronts + x * HALF + row)
    scale, logs = weigh(before, was_first)
    half_kib = HALF * LANES * 4 // 1024
    tile = reduce_group(3, scale, is_first, logs)
    tsend[...] = tile
    yexf[y] = tile
    for dy in range(1, xn):
        remote(tsend, yexf.at[y], y_send.at[1], y_recv.at[3], dev(s, x, around(y, dy, xn), z)).start()
    wait_kib(y_recv.at[3], (xn - 1) * half_kib)
    tlf[z, x] = tree(yexf[j] for j in range(xn))
    for dz, dx in offsets:
        where = dev(s, around(x, dx, xn), y, around(z, dz, zn))
        remote(tlf.at[z, x], tlf.at[z, x], y_send.at[2], tl_recv.at[3], where).start()
    is_first = outcome_rows(3, fronts, lambda row: s * fronts + row)
    for distance in range(reach + 1):
        wait_blocks(3, distance)
    wait_kib(tl_recv.at[3], len(offsets) * half_kib)
    total = jnp.concatenate([tree(tlf[j, g] for j in range(zn)) for g in range(xn)], axis=0)
    scale, logs = weigh(total, is_first)
    width = BLOCK // LANES
    stride = zn * width
    for g in range(xn):
        wide_scale = jnp.broadcast_to(scale[g * HALF : (g + 1) * HALF], (HALF, LANES))
        for j in range(zn):
            for c in range(width):
                rows_ref[pl.ds(g * HALF * stride + j * width + c, HALF, stride=stride), :] = (
                    stf[j, g, c] * wide_scale
                )
    lane = lax.broadcasted_iota(jnp.int32, (fronts, LANES), 1)
    row = lax.broadcasted_iota(jnp.int32, (fronts, LANES), 0)
    log_ref[...] = jnp.sum(jnp.where(lane == row, logs, 0.0), axis=0, keepdims=True)[:, :fronts]
    end_gather_sends(3)
    wait_kib(y_send.at[1], (xn - 1) * half_kib)
    wait_kib(y_send.at[2], len(offsets) * half_kib)


def shards(xn, zn, initial_rows, outcomes, tensors):
    fronts, _, rows_k = initial_rows.shape
    bond = xn * rows_k
    dma = pltpu.SemaphoreType.DMA
    vmem = pl.BlockSpec(memory_space=pltpu.VMEM)
    anywhere = pl.BlockSpec(memory_space=pl.ANY)
    f32 = jnp.float32
    lines = fronts * rows_k // LANES
    reach = zn // 2
    rows, logs = pl.pallas_call(
        functools.partial(kernel, xn, zn, float(bond)),
        out_shape=(
            jax.ShapeDtypeStruct((lines, LANES), f32),
            jax.ShapeDtypeStruct((1, fronts), f32),
        ),
        in_specs=[anywhere, vmem, anywhere],
        out_specs=(vmem, vmem),
        scratch_shapes=[
            pltpu.VMEM((2, 2, rows_k, BLOCK), f32),
            pltpu.VMEM((2, 2, rows_k, BLOCK), jnp.bfloat16),
            pltpu.VMEM((2, 2, rows_k, BLOCK), jnp.bfloat16),
            pltpu.VMEM((2, lines, LANES), f32),
            pltpu.VMEM((STEPS, xn, GROUP, 2 * BLOCK), f32),
            pltpu.VMEM((3, xn, GROUP, 2 * BLOCK), f32),
            pltpu.VMEM((xn, HALF, 2 * BLOCK), f32),
            pltpu.VMEM((3, zn, xn, 2, GROUP, LANES), f32),
            pltpu.VMEM((3, zn, GROUP, LANES), f32),
            pltpu.VMEM((zn, xn, 2, HALF, LANES), f32),
            pltpu.VMEM((zn, xn, HALF, LANES), f32),
            pltpu.VMEM((3, xn, GROUP, LANES), f32),
            pltpu.VMEM((xn, HALF, LANES), f32),
            pltpu.VMEM((3, GROUP, LANES), f32),
            pltpu.VMEM((HALF, LANES), f32),
            dma((2, max(1, rows_k // 512))),
            dma((3,)),
            dma((STEPS,)),
            dma((STEPS,)),
            dma((STEPS,)),
            dma((STEPS, reach + 1)),
            dma((3,)),
            dma((STEPS,)),
            dma((STEPS,)),
        ],
        compiler_params=pltpu.CompilerParams(
            collective_id=0, has_side_effects=True, vmem_limit_bytes=56 * 1024 * 1024
        ),
    )(initial_rows.reshape(lines, LANES), outcomes.T, tensors)
    return rows.reshape(fronts, 1, rows_k), logs.reshape(fronts)


def solution(mesh):
    xn = mesh.shape["narrow"]
    zn = mesh.shape["wide"] // xn
    return jax.shard_map(
        functools.partial(shards, xn, zn),
        mesh=mesh,
        in_specs=(P("site", "narrow", None), P(), P("site", None, "narrow", None, "wide")),
        out_specs=(P("site", "narrow", None), P("site")),
        check_vma=False,
    )
```

time: 79.5 us -> 76.9 us (0.967)
  local copies, waits for them, and re-layouts: 3.85 us -> 2.8 us
  other arithmetic: 1.04 us -> 0 us
    slice x1 -> x0, local copies, waits for them, and re-layouts: 1.49 us -> none  [shards(): return (rows, aux[:, 64])]
    broadcast_in_dim x1 -> x0, other arithmetic: 1.04 us -> none  [shards(): rows = (raw * aux[:, :1])[:, None, :]]
where the time goes in v2:
time: 76.9 us; the launch traced here: 76 us
  Pallas kernels  72.6 us (94%)
  local copies, waits for them, and re-layouts  2.8 us (4%)
    pallas_call x1, Pallas kernels, shards(): pl.pallas_call(functools.partial(kernel, xn, zn, float(bond)), out_shape=...  72.6 us
    unnamed x2, local copies, waits for them, and re-layouts  2.8 us

profile of v2, /device:TPU:8, one launch (start us, length us, event | category | flops | bytes accessed | tf_op | source)
XLA Modules:
  0.0 76.0 jit_solution(7200169380616176180)
XLA Ops:
  0.6 72.6 %shard_map.50 = (f32[512,128]{1,0:T(8,128)}, f32[1,32]{1,0:T(1,128)}) custom-call(f32[512,128]{1,0:T(8,128)} %bitcast.4, s32[4,64]{1,0:T(4,128)} %bitcast.6, f32[2,2,1,2048,256]{4,3,2,1,0:T(8,128)} %t_hbm.1), custom_call_target="tpu_custom_call" | custom-call | tf_op jit(solution)/shard_map/pallas_call | solution.py:393
  73.2 1.7 %copy.8 = f32[32,1,2048]{2,1,0:T(1,128)} copy(f32[32,1,2048]{2,1,0:T(1,128)} %bitcast.5) | data formatting | bytes 524288
  74.9 1.1 %copy.9 = f32[32]{0:T(128)} copy(f32[32]{0:T(128)} %bitcast.7) | data formatting | bytes 256

commit v3 on v2

v3 whole, which is shorter than its diff:
```python
import functools

import jax
import jax.numpy as jnp
from jax import lax
from jax.experimental import pallas as pl
from jax.experimental.pallas import tpu as pltpu
from jax.sharding import PartitionSpec as P

MESH = pl.DeviceIdType.MESH
EPSILON = 1e-06
STEPS = 4
BLOCK = 256
HALF = 8
LANES = 128


def split_value(value):
    high = value.astype(jnp.bfloat16)
    low = (value - high.astype(jnp.float32)).astype(jnp.bfloat16)
    return high, low


def ring_distance(offset, extent):
    return min(offset, extent - offset)


def kernel(
    xn,
    zn,
    bond,
    x_hbm,
    oc_ref,
    t_hbm,
    rows_ref,
    log_ref,
    t32,
    thi,
    tlo,
    xin,
    pfirst,
    psend,
    rsb,
    st,
    tl,
    tlf,
    yex,
    ysend,
    t_sem,
    t_send,
    t_recv,
    x_sem,
    rs_send,
    rs_recv,
    ag_send,
    ag_recv,
    y_send,
    y_recv,
    tl_recv,
):
    s = lax.axis_index("site")
    w = lax.axis_index("wide")
    y = lax.axis_index("narrow")
    x = lax.div(w, zn)
    z = lax.rem(w, zn)
    fronts = xn * HALF
    reach = zn // 2
    width = BLOCK // LANES
    stride = zn * width
    offsets = [(dz, dx) for dz in range(zn) for dx in range(xn) if dz or dx]
    offsets.sort(key=lambda o: -(ring_distance(o[0], zn) + ring_distance(o[1], xn)))
    across = sorted(range(xn), key=lambda d: -ring_distance(d, xn))

    def dev(site, xx, yy, zz):
        return (site, xx * zn + zz, yy)

    def around(value, offset, extent):
        return lax.rem(value + offset, extent)

    def remote(src, dst, send, recv, where):
        return pltpu.make_async_remote_copy(
            src_ref=src, dst_ref=dst, send_sem=send, recv_sem=recv, device_id=where, device_id_type=MESH
        )

    def wait_kib(sem, kib):
        view = xin.at[0, pl.ds(0, 2 * kib), :] if kib % 8 else t32.at[0, 0, pl.ds(0, kib), :]
        pltpu.make_async_copy(view, view, sem).wait()

    rows_k = zn * BLOCK
    t_chunk = min(rows_k, 512)
    chunks = rows_k // t_chunk
    partner = dev(around(s, 1, 2), x, y, z)

    def t_copy(local, c):
        rows = pl.ds(c * t_chunk, t_chunk)
        return pltpu.make_async_copy(
            t_hbm.at[local, :, 0, rows, :], t32.at[2 * s + local, :, rows, :], t_sem.at[local, c]
        )

    def lend(local, site, index):
        for c in range(chunks):
            rows = pl.ds(c * t_chunk, t_chunk)
            remote(
                t_hbm.at[local, :, 0, rows, :],
                t32.at[site, :, rows, :],
                t_send.at[index],
                t_recv.at[index],
                partner,
            ).start()

    def wait_site(sem):
        pltpu.make_async_copy(t32.at[0], t32.at[0], sem).wait()

    own_rows = pltpu.make_async_copy(x_hbm, xin.at[0], x_sem.at[0])
    partner_rows = remote(x_hbm, xin.at[1], x_sem.at[1], x_sem.at[2], partner)
    pl.when(s == 0)(own_rows.start)
    for local in range(2):
        for c in range(chunks):
            t_copy(local, c).start()

    barrier = pltpu.get_barrier_semaphore()
    peers = 0
    for ds in range(2):
        for dx in range(xn):
            for dy in range(xn):
                if ds or dx or dy:
                    where = dev(around(s, ds, 2), around(x, dx, xn), around(y, dy, xn), z)
                    pl.semaphore_signal(barrier, inc=1, device_id=where, device_id_type=MESH)
                    peers += 1
    for dz in range(1, zn):
        for dx in range(xn):
            where = dev(s, around(x, dx, xn), y, around(z, dz, zn))
            pl.semaphore_signal(barrier, inc=1, device_id=where, device_id_type=MESH)
            peers += 1

    def split_rows(site, start):
        for o in range(2):
            rows = pl.ds(start, BLOCK)
            high, low = split_value(t32[site, o, rows, :])
            thi[site, o, rows, :] = high
            tlo[site, o, rows, :] = low

    def split_site(site):
        for b in range(zn):
            split_rows(site, b * BLOCK)

    def block_product(lhs, site, start):
        high, low = split_value(lhs)
        both = jnp.concatenate([high, low], axis=0)
        n = lhs.shape[0]
        rows = pl.ds(start, BLOCK)
        out = []
        for o in range(2):
            t_high, t_low = thi[site, o, rows, :], tlo[site, o, rows, :]
            main = jnp.dot(both, t_high, preferred_element_type=jnp.float32)
            rest = jnp.dot(high, t_low, preferred_element_type=jnp.float32)
            out.append(main[:n] + (main[n:] + rest))
        return out

    each_part = HALF * 2 * BLOCK * 4 // 1024

    def reduce_sends(k, parts, core, maybe_here):
        for dg in across:
            g = around(x, dg, xn)
            src, dst = parts.at[g], rsb.at[k, y]
            copy = remote(src, dst, rs_send.at[k], rs_recv.at[k], dev(core, g, x, z))
            if dg == 0 and maybe_here:
                local = pltpu.make_async_copy(src, dst, rs_recv.at[k])
                pl.when(x == y)(local.start)
                pl.when(x != y)(copy.start)
            else:
                copy.start()

    def end_reduce_sends(k, count):
        pl.when(x == y)(lambda: wait_kib(rs_send.at[k], (count - 1) * each_part))
        pl.when(x != y)(lambda: wait_kib(rs_send.at[k], count * each_part))

    def outcome_rows(k, rows, first_row):
        line = oc_ref[k : k + 1, :].astype(jnp.float32)
        shape = (rows, oc_ref.shape[1])
        lane = lax.broadcasted_iota(jnp.int32, shape, 1)
        row = lax.broadcasted_iota(jnp.int32, shape, 0)
        picked = jnp.where(lane == row + first_row, jnp.broadcast_to(line, shape), 0.0)
        return jnp.sum(picked, axis=1, keepdims=True) < 0.5

    def weigh(total, is_first):
        first, second = total[:, 0:1], total[:, 32:33]
        both_mean = (first + second) / (2.0 * bond)
        kept_square = jnp.where(is_first, first, second)
        scale = lax.rsqrt(both_mean + EPSILON)
        ratio = jnp.log(kept_square / bond + EPSILON) - jnp.log(both_mean + EPSILON)
        return scale, total[:, 64:65] + ratio

    def tree(items):
        items = list(items)
        while len(items) > 1:
            items = [sum(items[i : i + 2][1:], items[i]) for i in range(0, len(items), 2)]
        return items[0]

    def reduce_group(k, scale, is_first, log_sum):
        wait_kib(rs_recv.at[k], xn * each_part)
        total = tree(rsb[k, j] for j in range(xn))
        if scale is not None:
            total = total * scale
        first, second = total[:, :BLOCK], total[:, BLOCK:]
        kept = jnp.where(is_first, first, second)
        block = st.at[k, z, x]
        block[0] = kept[:, :LANES]
        block[1] = kept[:, LANES:]
        for dz, dx in offsets:
            copy = remote(
                block,
                block,
                ag_send.at[k],
                ag_recv.at[k, ring_distance(dz, zn)],
                dev(s, around(x, dx, xn), y, around(z, dz, zn)),
            )
            copy.start()
        square_first = jnp.sum(first * first, axis=1, keepdims=True)
        square_second = jnp.sum(second * second, axis=1, keepdims=True)
        lane = lax.broadcasted_iota(jnp.int32, (HALF, LANES), 1)
        carried = jnp.where((lane >= 64) & (y == 0) & (z == 0), log_sum, 0.0)
        return jnp.where(lane < 32, square_first, jnp.where(lane < 64, square_second, carried))

    each_block = HALF * BLOCK * 4 // 1024

    def end_gather_sends(k):
        wait_kib(ag_send.at[k], len(offsets) * each_block)

    def wait_blocks(k, distance):
        count = sum(1 for dz, dx in offsets if ring_distance(dz, zn) == distance)
        wait_kib(ag_recv.at[k, distance], count * each_block)

    tile_kib = HALF * LANES * 4 // 1024

    def spread_tile(k, tile):
        tl[k, z] = tile
        for dz in range(1, zn):
            copy = remote(tl.at[k, z], tl.at[k, z], y_send.at[0], tl_recv.at[k], dev(s, x, y, around(z, dz, zn)))
            copy.start()

    def pass_tile(k, total):
        ysend[k] = total
        yex[k, y] = total
        for dy in range(1, xn):
            where = dev(s, x, around(y, dy, xn), z)
            remote(ysend.at[k], yex.at[k, y], y_send.at[1], y_recv.at[k], where).start()

    def tile_total(k):
        wait_kib(y_recv.at[k], (xn - 1) * tile_kib)
        return tree(yex[k, j] for j in range(xn))

    def gathered_product(k):
        total = None
        for distance in range(reach + 1):
            wait_blocks(k, distance)
            for dz in sorted({distance, (zn - distance) % zn}):
                z2 = around(z, dz, zn)
                lhs = jnp.concatenate(
                    [jnp.concatenate([st[k, z2, g, 0], st[k, z2, g, 1]], axis=1) for g in range(xn)], axis=0
                )
                out = block_product(lhs, k + 1, pl.multiple_of(z2 * BLOCK, BLOCK))
                total = out if total is None else [total[0] + out[0], total[1] + out[1]]
        for g in range(xn):
            for o in range(2):
                psend[k, g, :, o * BLOCK : (o + 1) * BLOCK] = total[o][g * HALF : (g + 1) * HALF]

    @pl.when(s == 0)
    def _():
        own_rows.wait()
        for c in range(chunks):
            t_copy(0, c).wait()
            for b in range(t_chunk // BLOCK):
                split_rows(0, c * t_chunk + b * BLOCK)

    pl.semaphore_wait(barrier, peers)

    @pl.when(s == 0)
    def _():
        partner_rows.wait_recv()
        total = None
        for kb in range(zn):
            pieces = [
                jnp.concatenate(
                    [
                        xin[f, pl.ds(g * HALF * stride + kb * width + c, HALF, stride=stride), :]
                        for c in range(width)
                    ],
                    axis=1,
                )
                for f in range(2)
                for g in range(xn)
            ]
            out = block_product(jnp.concatenate(pieces, axis=0), 0, kb * BLOCK)
            total = out if total is None else [total[0] + out[0], total[1] + out[1]]
        for f in range(2):
            for g in range(xn):
                row = (f * xn + g) * HALF
                for o in range(2):
                    pfirst[f, g, :, o * BLOCK : (o + 1) * BLOCK] = total[o][row : row + HALF]
        reduce_sends(0, pfirst.at[1], 1, False)
        reduce_sends(0, pfirst.at[0], 0, True)
        lend(1, 1, 0)
        for c in range(chunks):
            t_copy(1, c).wait()
        split_site(1)

    @pl.when(s == 1)
    def _():
        partner_rows.start()
        lend(0, 2, 1)
        for local in range(2):
            for c in range(chunks):
                t_copy(local, c).wait()
            split_site(2 + local)

    own_first = s * fronts + x * HALF
    is_first = outcome_rows(0, HALF, own_first)
    spread_tile(0, reduce_group(0, None, is_first, 0.0))

    @pl.when(s == 1)
    def _():
        lend(1, 3, 2)
        wait_site(t_recv.at[0])
        split_site(1)

    logs = jnp.zeros((HALF, 1), jnp.float32)
    for k in range(1, STEPS):
        gathered_product(k - 1)
        reduce_sends(k, psend.at[k - 1], s, True)
        wait_kib(tl_recv.at[k - 1], (zn - 1) * tile_kib)
        pass_tile(k - 1, tree(tl[k - 1, j] for j in range(zn)))
        if k < STEPS - 1:

            @pl.when(s == 0)
            def _():
                wait_site(t_recv.at[k])
                split_site(k + 1)

        was_first, is_first = is_first, outcome_rows(k, HALF, own_first)
        scale, more = weigh(tile_total(k - 1), was_first)
        logs = logs + more
        tile = reduce_group(k, scale, is_first, logs if k == STEPS - 1 else 0.0)
        if k < STEPS - 1:
            spread_tile(k, tile)

    last = STEPS - 1
    pass_tile(last, tile)
    tlf[z, x] = tile_total(last)
    for dz, dx in offsets:
        where = dev(s, around(x, dx, xn), y, around(z, dz, zn))
        remote(tlf.at[z, x], tlf.at[z, x], y_send.at[2], tl_recv.at[last], where).start()
    is_first = outcome_rows(last, fronts, s * fronts)
    for distance in range(reach + 1):
        wait_blocks(last, distance)
    wait_kib(tl_recv.at[last], len(offsets) * tile_kib)
    total = jnp.concatenate([tree(tlf[j, g] for j in range(zn)) for g in range(xn)], axis=0)
    scale, logs = weigh(total, is_first)
    for g in range(xn):
        wide_scale = jnp.broadcast_to(scale[g * HALF : (g + 1) * HALF], (HALF, LANES))
        for j in range(zn):
            for c in range(width):
                rows_ref[pl.ds(g * HALF * stride + j * width + c, HALF, stride=stride), :] = (
                    st[last, j, g, c] * wide_scale
                )
    lane = lax.broadcasted_iota(jnp.int32, (fronts, LANES), 1)
    row = lax.broadcasted_iota(jnp.int32, (fronts, LANES), 0)
    log_ref[...] = jnp.sum(jnp.where(lane == row, logs, 0.0), axis=0, keepdims=True)[:, :fronts]

    @pl.when(s == 0)
    def _():
        end_reduce_sends(0, 2 * xn)
        wait_site(t_send.at[0])

    @pl.when(s == 1)
    def _():
        partner_rows.wait_send()
        wait_site(t_send.at[1])
        wait_site(t_send.at[2])

    for k in range(STEPS):
        if k:
            end_reduce_sends(k, xn)
        end_gather_sends(k)
    wait_kib(y_send.at[0], (STEPS - 1) * (zn - 1) * tile_kib)
    wait_kib(y_send.at[1], STEPS * (xn - 1) * tile_kib)
    wait_kib(y_send.at[2], len(offsets) * tile_kib)


def shards(xn, zn, initial_rows, outcomes, tensors):
    fronts, _, rows_k = initial_rows.shape
    bond = xn * rows_k
    dma = pltpu.SemaphoreType.DMA
    vmem = pl.BlockSpec(memory_space=pltpu.VMEM)
    anywhere = pl.BlockSpec(memory_space=pl.ANY)
    f32 = jnp.float32
    lines = fronts * rows_k // LANES
    reach = zn // 2
    rows, logs = pl.pallas_call(
        functools.partial(kernel, xn, zn, float(bond)),
        out_shape=(
            jax.ShapeDtypeStruct((lines, LANES), f32),
            jax.ShapeDtypeStruct((1, fronts), f32),
        ),
        in_specs=[anywhere, vmem, anywhere],
        out_specs=(vmem, vmem),
        scratch_shapes=[
            pltpu.VMEM((STEPS, 2, rows_k, BLOCK), f32),
            pltpu.VMEM((STEPS, 2, rows_k, BLOCK), jnp.bfloat16),
            pltpu.VMEM((STEPS, 2, rows_k, BLOCK), jnp.bfloat16),
            pltpu.VMEM((2, lines, LANES), f32),
            pltpu.VMEM((2, xn, HALF, 2 * BLOCK), f32),
            pltpu.VMEM((STEPS - 1, xn, HALF, 2 * BLOCK), f32),
            pltpu.VMEM((STEPS, xn, HALF, 2 * BLOCK), f32),
            pltpu.VMEM((STEPS, zn, xn, 2, HALF, LANES), f32),
            pltpu.VMEM((STEPS - 1, zn, HALF, LANES), f32),
            pltpu.VMEM((zn, xn, HALF, LANES), f32),
            pltpu.VMEM((STEPS, xn, HALF, LANES), f32),
            pltpu.VMEM((STEPS, HALF, LANES), f32),
            dma((2, max(1, rows_k // 512))),
            dma((3,)),
            dma((3,)),
            dma((3,)),
            dma((STEPS,)),
            dma((STEPS,)),
            dma((STEPS,)),
            dma((STEPS, reach + 1)),
            dma((3,)),
            dma((STEPS,)),
            dma((STEPS,)),
        ],
        compiler_params=pltpu.CompilerParams(
            collective_id=0, has_side_effects=True, vmem_limit_bytes=56 * 1024 * 1024
        ),
    )(initial_rows.reshape(lines, LANES), outcomes.T, tensors)
    return rows.reshape(fronts, 1, rows_k), logs.reshape(fronts)


def solution(mesh):
    xn = mesh.shape["narrow"]
    zn = mesh.shape["wide"] // xn
    return jax.shard_map(
        functools.partial(shards, xn, zn),
        mesh=mesh,
        in_specs=(P("site", "narrow", None), P(), P("site", None, "narrow", None, "wide")),
        out_specs=(P("site", "narrow", None), P("site")),
        check_vma=False,
    )
```

time: 76.9 us -> 70.3 us (0.914)
  Pallas kernels: 72.6 us -> 66.2 us
    pallas_call x1, Pallas kernels: 72.6 us -> 66.2 us  [shards(): pl.pallas_call(functools.partial(kernel, xn, zn, float(bond)), out_shape=...]
where the time goes in v3:
time: 70.3 us; the launch traced here: 69.7 us
  Pallas kernels  66.2 us (94%)
  local copies, waits for them, and re-layouts  2.8 us (4%)
    pallas_call x1, Pallas kernels, shards(): pl.pallas_call(functools.partial(kernel, xn, zn, float(bond)), out_shape=...  66.2 us
    unnamed x2, local copies, waits for them, and re-layouts  2.8 us

profile of v3, /device:TPU:8, one launch (start us, length us, event | category | flops | bytes accessed | tf_op | source)
XLA Modules:
  0.0 69.7 jit_solution(7618884180199711102)
XLA Ops:
  0.6 66.2 %shard_map.50 = (f32[512,128]{1,0:T(8,128)}, f32[1,32]{1,0:T(1,128)}) custom-call(f32[512,128]{1,0:T(8,128)} %bitcast.4, s32[4,64]{1,0:T(4,128)} %bitcast.6, f32[2,2,1,2048,256]{4,3,2,1,0:T(8,128)} %t_hbm.1), custom_call_target="tpu_custom_call" | custom-call | tf_op jit(solution)/shard_map/pallas_call | solution.py:399
  66.9 1.7 %copy.8 = f32[32,1,2048]{2,1,0:T(1,128)} copy(f32[32,1,2048]{2,1,0:T(1,128)} %bitcast.5) | data formatting | bytes 524288
  68.5 1.1 %copy.9 = f32[32]{0:T(128)} copy(f32[32]{0:T(128)} %bitcast.7) | data formatting | bytes 256

commit v4 on v3

--- a/solution.py
+++ b/solution.py
@@ -10,6 +10,7 @@
 MESH = pl.DeviceIdType.MESH
 EPSILON = 1e-06
 STEPS = 4
+RELAYED = (1,)
 BLOCK = 256
 HALF = 8
 LANES = 128
@@ -57,6 +58,7 @@
     y_send,
     y_recv,
     tl_recv,
+    relay_recv,
 ):
     s = lax.axis_index("site")
     w = lax.axis_index("wide")
@@ -112,8 +114,8 @@
         pltpu.make_async_copy(t32.at[0], t32.at[0], sem).wait()
 
     own_rows = pltpu.make_async_copy(x_hbm, xin.at[0], x_sem.at[0])
-    partner_rows = remote(x_hbm, xin.at[1], x_sem.at[1], x_sem.at[2], partner)
-    pl.when(s == 0)(own_rows.start)
+    partner_rows = remote(xin.at[0], xin.at[1], x_sem.at[1], x_sem.at[2], partner)
+    own_rows.start()
     for local in range(2):
         for c in range(chunks):
             t_copy(local, c).start()
@@ -144,14 +146,16 @@
         for b in range(zn):
             split_rows(site, b * BLOCK)
 
-    def block_product(lhs, site, start):
+    def block_product(lhs, site, starts):
         high, low = split_value(lhs)
         both = jnp.concatenate([high, low], axis=0)
         n = lhs.shape[0]
-        rows = pl.ds(start, BLOCK)
         out = []
         for o in range(2):
-            t_high, t_low = thi[site, o, rows, :], tlo[site, o, rows, :]
+            t_high, t_low = (
+                jnp.concatenate([half[site, o, pl.ds(start, BLOCK), :] for start in starts], axis=0)
+                for half in (thi, tlo)
+            )
             main = jnp.dot(both, t_high, preferred_element_type=jnp.float32)
             rest = jnp.dot(high, t_low, preferred_element_type=jnp.float32)
             out.append(main[:n] + (main[n:] + rest))
@@ -207,15 +211,16 @@
         block = st.at[k, z, x]
         block[0] = kept[:, :LANES]
         block[1] = kept[:, LANES:]
-        for dz, dx in offsets:
-            copy = remote(
-                block,
-                block,
-                ag_send.at[k],
-                ag_recv.at[k, ring_distance(dz, zn)],
-                dev(s, around(x, dx, xn), y, around(z, dz, zn)),
-            )
-            copy.start()
+        for dz, dx in sorted(offsets, key=lambda o: ring_distance(o[0], zn) not in RELAYED):
+            distance = ring_distance(dz, zn)
+            if distance in RELAYED:
+                if dx:
+                    continue
+                arrived = relay_recv.at[k, distance]
+            else:
+                arrived = ag_recv.at[k, distance]
+            where = dev(s, around(x, dx, xn), y, around(z, dz, zn))
+            remote(block, block, ag_send.at[k], arrived, where).start()
         square_first = jnp.sum(first * first, axis=1, keepdims=True)
         square_second = jnp.sum(second * second, axis=1, keepdims=True)
         lane = lax.broadcasted_iota(jnp.int32, (HALF, LANES), 1)
@@ -227,8 +232,21 @@
     def end_gather_sends(k):
         wait_kib(ag_send.at[k], len(offsets) * each_block)
 
+    def relay(k, low, high):
+        for distance in range(low, high + 1):
+            if distance in RELAYED:
+                offset_pair = sorted({distance, zn - distance})
+                wait_kib(relay_recv.at[k, distance], len(offset_pair) * each_block)
+                for dz in offset_pair:
+                    block = st.at[k, around(z, dz, zn), x]
+                    for dx in across[:-1]:
+                        where = dev(s, around(x, dx, xn), y, z)
+                        remote(block, block, ag_send.at[k], ag_recv.at[k, distance], where).start()
+
     def wait_blocks(k, distance):
         count = sum(1 for dz, dx in offsets if ring_distance(dz, zn) == distance)
+        if distance in RELAYED:
+            count = count * (xn - 1) // xn
         wait_kib(ag_recv.at[k, distance], count * each_block)
 
     tile_kib = HALF * LANES * 4 // 1024
@@ -254,13 +272,16 @@
         total = None
         for distance in range(reach + 1):
             wait_blocks(k, distance)
-            for dz in sorted({distance, (zn - distance) % zn}):
-                z2 = around(z, dz, zn)
-                lhs = jnp.concatenate(
-                    [jnp.concatenate([st[k, z2, g, 0], st[k, z2, g, 1]], axis=1) for g in range(xn)], axis=0
-                )
-                out = block_product(lhs, k + 1, pl.multiple_of(z2 * BLOCK, BLOCK))
-                total = out if total is None else [total[0] + out[0], total[1] + out[1]]
+            places = [around(z, dz, zn) for dz in sorted({distance, (zn - distance) % zn})]
+            lhs = jnp.concatenate(
+                [
+                    jnp.concatenate([st[k, z2, g, c] for z2 in places for c in range(width)], axis=1)
+                    for g in range(xn)
+                ],
+                axis=0,
+            )
+            out = block_product(lhs, k + 1, [pl.multiple_of(z2 * BLOCK, BLOCK) for z2 in places])
+            total = out if total is None else [total[0] + out[0], total[1] + out[1]]
         for g in range(xn):
             for o in range(2):
                 psend[k, g, :, o * BLOCK : (o + 1) * BLOCK] = total[o][g * HALF : (g + 1) * HALF]
@@ -291,7 +312,7 @@
                 for f in range(2)
                 for g in range(xn)
             ]
-            out = block_product(jnp.concatenate(pieces, axis=0), 0, kb * BLOCK)
+            out = block_product(jnp.concatenate(pieces, axis=0), 0, [kb * BLOCK])
             total = out if total is None else [total[0] + out[0], total[1] + out[1]]
         for f in range(2):
             for g in range(xn):
@@ -307,6 +328,7 @@
 
     @pl.when(s == 1)
     def _():
+        own_rows.wait()
         partner_rows.start()
         lend(0, 2, 1)
         for local in range(2):
@@ -317,6 +339,7 @@
     own_first = s * fronts + x * HALF
     is_first = outcome_rows(0, HALF, own_first)
     spread_tile(0, reduce_group(0, None, is_first, 0.0))
+    relay(0, 1, reach)
 
     @pl.when(s == 1)
     def _():
@@ -343,13 +366,16 @@
         tile = reduce_group(k, scale, is_first, logs if k == STEPS - 1 else 0.0)
         if k < STEPS - 1:
             spread_tile(k, tile)
+            relay(k, 1, reach)
 
     last = STEPS - 1
     pass_tile(last, tile)
+    relay(last, 1, 1)
     tlf[z, x] = tile_total(last)
     for dz, dx in offsets:
         where = dev(s, around(x, dx, xn), y, around(z, dz, zn))
         remote(tlf.at[z, x], tlf.at[z, x], y_send.at[2], tl_recv.at[last], where).start()
+    relay(last, 2, reach)
     is_first = outcome_rows(last, fronts, s * fronts)
     for distance in range(reach + 1):
         wait_blocks(last, distance)
@@ -387,6 +413,17 @@
     wait_kib(y_send.at[2], len(offsets) * tile_kib)
 
 
+def deliver(rows_ref, log_ref, rows_out, log_out, sem):
+    copies = (
+        pltpu.make_async_copy(rows_ref, rows_out, sem.at[0]),
+        pltpu.make_async_copy(log_ref, log_out, sem.at[1]),
+    )
+    for copy in copies:
+        copy.start()
+    for copy in copies:
+        copy.wait()
+
+
 def shards(xn, zn, initial_rows, outcomes, tensors):
     fronts, _, rows_k = initial_rows.shape
     bond = xn * rows_k
@@ -399,8 +436,8 @@
     rows, logs = pl.pallas_call(
         functools.partial(kernel, xn, zn, float(bond)),
         out_shape=(
-            jax.ShapeDtypeStruct((lines, LANES), f32),
-            jax.ShapeDtypeStruct((1, fronts), f32),
+            pltpu.VMEM((lines, LANES), f32),
+            pltpu.VMEM((1, fronts), f32),
         ),
         in_specs=[anywhere, vmem, anywhere],
         out_specs=(vmem, vmem),
@@ -428,11 +465,22 @@
             dma((3,)),
             dma((STEPS,)),
             dma((STEPS,)),
+            dma((STEPS, reach + 1)),
         ],
         compiler_params=pltpu.CompilerParams(
             collective_id=0, has_side_effects=True, vmem_limit_bytes=56 * 1024 * 1024
         ),
     )(initial_rows.reshape(lines, LANES), outcomes.T, tensors)
+    rows, logs = pl.pallas_call(
+        deliver,
+        out_shape=(
+            jax.ShapeDtypeStruct((lines, LANES), f32),
+            jax.ShapeDtypeStruct((1, fronts), f32),
+        ),
+        in_specs=[vmem, vmem],
+        out_specs=(anywhere, anywhere),
+        scratch_shapes=[dma((2,))],
+    )(pltpu.with_memory_space_constraint(rows, pltpu.VMEM), pltpu.with_memory_space_constraint(logs, pltpu.VMEM))
     return rows.reshape(fronts, 1, rows_k), logs.reshape(fronts)
 
 

time: 70.3 us -> 66.9 us (0.952)
  local copies, waits for them, and re-layouts: 2.8 us -> 0 us
    unnamed x2 -> x0, local copies, waits for them, and re-layouts: 2.8 us -> none
    pallas_call x1, Pallas kernels: 66.2 us -> 65.4 us  [shards(): pl.pallas_call(functools.partial(kernel, xn, zn, float(bond)), out_shape=...]
    pallas_call x0 -> x1, Pallas kernels: none -> 0.72 us  [shards(): pl.pallas_call(deliver, out_shape=(jax.ShapeDtypeStruct((lines, LANES), f...]
where the time goes in v4:
time: 66.9 us; the launch traced here: 66.7 us
  Pallas kernels  66.1 us (99%)
    pallas_call x1, Pallas kernels, shards(): pl.pallas_call(functools.partial(kernel, xn, zn, float(bond)), out_shape=...  65.4 us

profile of v4, /device:TPU:8, one launch (start us, length us, event | category | flops | bytes accessed | tf_op | source)
XLA Modules:
  0.0 66.7 jit_solution(13805428263309334342)
XLA Ops:
  0.6 65.4 %shard_map.50 = (f32[512,128]{1,0:T(8,128)S(1)}, f32[1,32]{1,0:T(1,128)S(1)}) custom-call(f32[512,128]{1,0:T(8,128)} %bitcast.4, s32[4,64]{1,0:T(4,128)} %bitcast.5, f32[2,2,1,2048,256]{4,3,2,1,0:T(8,128)} %t_hbm.1), custom_call_target="tpu_custom_call" | custom-call | tf_op jit(solution)/shard_map/pallas_call | solution.py:436
  66.0 0.7 %shard_map.51 = (f32[512,128]{1,0:T(8,128)}, f32[1,32]{1,0:T(1,128)}) custom-call(f32[512,128]{1,0:T(8,128)S(1)} %get-tuple-element.6.rows_ref, f32[1,32]{1,0:T(1,128)S(1)} %get-tuple-element.7.log_ref), custom_call_target="tpu_custom_call" | custom-call | tf_op jit(solution)/shard_map/pallas_call | solution.py:474

commit v5 on v4

--- a/solution.py
+++ b/solution.py
@@ -70,7 +70,7 @@
     width = BLOCK // LANES
     stride = zn * width
     offsets = [(dz, dx) for dz in range(zn) for dx in range(xn) if dz or dx]
-    offsets.sort(key=lambda o: -(ring_distance(o[0], zn) + ring_distance(o[1], xn)))
+    offsets.sort(key=lambda o: (-(ring_distance(o[0], zn) + 2 * ring_distance(o[1], xn)), o[0]))
     across = sorted(range(xn), key=lambda d: -ring_distance(d, xn))
 
     def dev(site, xx, yy, zz):
@@ -216,7 +216,7 @@
             if distance in RELAYED:
                 if dx:
                     continue
-                arrived = relay_recv.at[k, distance]
+                arrived = relay_recv.at[k]
             else:
                 arrived = ag_recv.at[k, distance]
             where = dev(s, around(x, dx, xn), y, around(z, dz, zn))
@@ -236,7 +236,7 @@
         for distance in range(low, high + 1):
             if distance in RELAYED:
                 offset_pair = sorted({distance, zn - distance})
-                wait_kib(relay_recv.at[k, distance], len(offset_pair) * each_block)
+                wait_kib(relay_recv.at[k], len(offset_pair) * each_block)
                 for dz in offset_pair:
                     block = st.at[k, around(z, dz, zn), x]
                     for dx in across[:-1]:
@@ -465,7 +465,7 @@
             dma((3,)),
             dma((STEPS,)),
             dma((STEPS,)),
-            dma((STEPS, reach + 1)),
+            dma((STEPS,)),
         ],
         compiler_params=pltpu.CompilerParams(
             collective_id=0, has_side_effects=True, vmem_limit_bytes=56 * 1024 * 1024

time: 66.9 us -> 66.8 us (level)
  no operation moved by 1% of the time
where the time goes in v5:
time: 66.8 us; the launch traced here: 66.7 us
  Pallas kernels  66.1 us (99%)
    pallas_call x1, Pallas kernels, shards(): pl.pallas_call(functools.partial(kernel, xn, zn, float(bond)), out_shape=...  65.4 us

profile of v5, /device:TPU:8, one launch (start us, length us, event | category | flops | bytes accessed | tf_op | source)
XLA Modules:
  0.0 66.7 jit_solution(17894767247771420480)
XLA Ops:
  0.6 65.4 %shard_map.50 = (f32[512,128]{1,0:T(8,128)S(1)}, f32[1,32]{1,0:T(1,128)S(1)}) custom-call(f32[512,128]{1,0:T(8,128)} %bitcast.4, s32[4,64]{1,0:T(4,128)} %bitcast.5, f32[2,2,1,2048,256]{4,3,2,1,0:T(8,128)} %t_hbm.1), custom_call_target="tpu_custom_call" | custom-call | tf_op jit(solution)/shard_map/pallas_call | solution.py:436
  66.0 0.7 %shard_map.51 = (f32[512,128]{1,0:T(8,128)}, f32[1,32]{1,0:T(1,128)}) custom-call(f32[512,128]{1,0:T(8,128)S(1)} %get-tuple-element.6.rows_ref, f32[1,32]{1,0:T(1,128)S(1)} %get-tuple-element.7.log_ref), custom_call_target="tpu_custom_call" | custom-call | tf_op jit(solution)/shard_map/pallas_call | solution.py:474
